TPU v7x, 32 devices: a whole 2x2x4 slice. The times are simulated.
32 devices in a mesh: grp: 2 (over y), img: 4 (over z), sub: 2 (over x), cls: 2 (over core).
Axes of the slice: x: 2, y: 2, z: 4, core: 2. Of those that a mesh axis runs over, the one named last changes fastest.
Arguments:
- images: bfloat16 [4096, 3072], P(('grp', 'img', 'sub', 'cls')), parts along dimension 0, may hold values from -10 to 10
- labels: int32 [4096], P(('grp', 'img', 'sub', 'cls')), parts along dimension 0, may hold values from 0 to 999
- seeds: int32 [128], replicated, may hold values from 0 to 46336
Outputs:
- rfactor: float32 [1024, 512], P('grp'), parts along dimension 0
- projections: float32 [1024, 1000], P('grp', 'cls'), parts along dimension 0
There are 2 independent parts, one for each index of `grp`. A program takes and returns all parts, laid end to end along the dimension named above; an argument that names none is the same for every part. Nothing has to cross between parts.
All inputs are finite; a program needn't handle non-finite values.
Results may differ from a plain program's by a relative error of at most 0.0058.
Values sent between devices are 32-bit elements; how exact they have to be, the bound alone decides.
A program may use at most 128 MiB of HBM per device.

v0:
```python
import math

import jax
import jax.numpy as jnp
from jax import lax
from jax.experimental import pallas as pl
from jax.experimental.pallas import tpu as pltpu
from jax.sharding import PartitionSpec as P

CLASSES = 1000
RIDGE = 0.001
PANEL = 128
STRIP = 32
GATHER_LIMIT = 16 * 1024 * 1024
HIGHEST = lax.Precision.HIGHEST
MESH = pl.DeviceIdType.MESH


def pieces(value):
    first = value.astype(jnp.bfloat16).astype(jnp.float32)
    rest = value - first
    second = rest.astype(jnp.bfloat16).astype(jnp.float32)
    return first, second, rest - second


def product(left, right, left_dim, right_dim):
    l1, l2, l3 = pieces(left)
    r1, r2, r3 = pieces(right)
    lefts = jnp.concatenate([l1, l1, l2, l1, l3, l2], axis=left_dim).astype(jnp.bfloat16)
    rights = jnp.concatenate([r1, r2, r1, r3, r1, r2], axis=right_dim).astype(jnp.bfloat16)
    over = (((left_dim,), (right_dim,)), ((), ()))
    return lax.dot_general(lefts, rights, over, preferred_element_type=jnp.float32)


def factor_block(work):
    tiles = STRIP // 8
    sub = lax.broadcasted_iota(jnp.int32, (8, PANEL), 0)

    def spread(tile, row):
        return jnp.broadcast_to(tile[row:row + 1, :], (8, tile.shape[1]))

    def double(tile):
        return jnp.concatenate([tile, tile], axis=1)

    for base in range(0, PANEL, STRIP):
        rows = [work[base + 8 * h:base + 8 * h + 8, :] for h in range(tiles)]
        cols = {}
        for j in range(STRIP):
            for h in range(j // 8, tiles):
                cols[j, h] = jnp.broadcast_to(rows[h][:, base + j:base + j + 1], (8, PANEL))
        scale = [None] * tiles
        for k in range(0, STRIP, 2):
            own, row = divmod(k, 8)
            one = spread(cols[k, own], row)
            cross = spread(cols[k, own], row + 1)
            two = spread(cols[k + 1, own], row + 1)
            det = one * two - cross * cross
            one_inverse = 1.0 / one
            two_inverse = one / det
            ratio = cross * one_inverse
            paired = jnp.where(sub > row, det * one_inverse, one)
            scale[own] = paired if scale[own] is None else jnp.where(sub >= row, paired, scale[own])
            first, second, rest = {}, {}, {}
            for h in range(own, tiles):
                first[h] = cols[k, h] * one_inverse
                rest[h] = cols[k + 1, h] - first[h] * cross
                second[h] = rest[h] * two_inverse
                if h == own:
                    first[h] = jnp.where(sub > row, first[h], 0.0)
                    second[h] = jnp.where(sub > row + 1, second[h], 0.0)
            for j in range(k + 2, STRIP):
                peer, place = divmod(j, 8)
                entry = spread(cols[k, peer], place)
                other = spread(rest[peer], place)
                for h in range(peer, tiles):
                    cols[j, h] = cols[j, h] - first[h] * entry - second[h] * other
            line = spread(rows[own], row)
            next_line = spread(rows[own], row + 1) - double(ratio) * line
            for h in range(own, tiles):
                rows[h] = rows[h] - double(first[h]) * line - double(second[h]) * next_line
        for h in range(tiles):
            rows[h] = rows[h] * double(lax.rsqrt(scale[h]))
            work[base + 8 * h:base + 8 * h + 8, :] = rows[h]
        low = base + STRIP
        if low < PANEL:
            strip = jnp.concatenate(rows, axis=0)
            work[low:, :] = work[low:, :] - product(strip[:, low:PANEL], strip, 0, 0)


def factor_kernel(gram, sums, rfactor, projections, square, solved, work, sems):
    order = gram.shape[0]
    lane = lax.broadcasted_iota(jnp.int32, (PANEL, PANEL), 1)
    down = lax.broadcasted_iota(jnp.int32, (PANEL, PANEL), 0)
    square[...] = gram[...]
    solved[...] = sums[...]
    copies = []
    for number, base in enumerate(range(0, order, PANEL)):
        end = base + PANEL
        work[:, :PANEL] = square[base:end, base:end]
        work[:, PANEL:] = (lane == down).astype(jnp.float32)
        factor_block(work)
        inverse = work[:, PANEL:]
        square[base:end, base:end] = jnp.where(lane >= down, work[:, :PANEL], 0.0)
        if base:
            square[base:end, :base] = jnp.zeros((PANEL, base), jnp.float32)
        answer = product(solved[:, base:end], inverse, 1, 1)
        solved[:, base:end] = answer
        if end < order:
            panel = product(inverse, square[base:end, end:], 1, 0)
            square[base:end, end:] = panel
            for top in range(end, order, PANEL):
                square[top:top + PANEL, top:] = square[top:top + PANEL, top:] - product(panel[:, top - end:top - end + PANEL], panel[:, top - end:], 0, 0)
            solved[:, end:] = solved[:, end:] - product(answer, panel, 1, 0)
        copies.append(pltpu.make_async_copy(square.at[pl.ds(base, PANEL)], rfactor.at[pl.ds(base, PANEL)], sems.at[0, number]))
        copies.append(pltpu.make_async_copy(solved.at[:, pl.ds(base, PANEL)], projections.at[:, pl.ds(base, PANEL)], sems.at[1, number]))
        copies[-2].start()
        copies[-1].start()
    for copy in copies:
        copy.wait()


def factor(gram, sums):
    vmem = pl.BlockSpec(memory_space=pltpu.VMEM)
    order = gram.shape[0]
    return pl.pallas_call(
        factor_kernel,
        out_shape=(jax.ShapeDtypeStruct(gram.shape, jnp.float32), jax.ShapeDtypeStruct(sums.shape, jnp.float32)),
        in_specs=[vmem, vmem],
        out_specs=(pl.BlockSpec(memory_space=pl.ANY),) * 2,
        scratch_shapes=[
            pltpu.VMEM(gram.shape, jnp.float32),
            pltpu.VMEM(sums.shape, jnp.float32),
            pltpu.VMEM((PANEL, 2 * PANEL), jnp.float32),
            pltpu.SemaphoreType.DMA((2, order // PANEL)),
        ],
        compiler_params=pltpu.CompilerParams(vmem_limit_bytes=16 * 1024 * 1024),
        name="factor",
    )(gram, sums)


def features_kernel(images, seeds, labels, block, stack, spread, bank):
    count, pixels = images.shape
    plane = pixels // 3
    windows = (plane - 256) // 128 + 1
    lead = bank.shape[1] - 768
    down = lax.broadcasted_iota(jnp.int32, (8, 128), 0)
    seed = jnp.broadcast_to(seeds[...], (8, 128))
    spread[...] = jnp.zeros_like(spread)
    for c in range(3):
        for a in range(6):
            index = 36 * c + 6 * a + down
            first = lax.rem(seed * 7919 + index * 104729, 46337)
            second = lax.rem(first * first + seed, 46337)
            values = (second.astype(jnp.float32) / 46337.0 - 0.5) * math.sqrt(12.0 / 108.0)
            values = jnp.where(down < 6, values, 0.0)
            for shift in range(8):
                top = lead + 256 * c + 32 * a + 2 * shift
                spread[shift, top:top + 8, :] = values
    for shift in range(8):
        bank[shift] = spread[shift].astype(jnp.bfloat16)
    for m in range(windows):
        for c in range(3):
            stack[m * count:(m + 1) * count, 256 * c:256 * c + 256] = images[:, plane * c + 128 * m:plane * c + 128 * m + 256]

    def laid(row, column):
        skip, shift = divmod(2 * column, 16)
        top = lead - 64 * row - 16 * skip
        return bank[shift // 2, top:top + 768, :]

    total = [None] * 4
    for row in range(2):
        for column in range(0, 14, 2):
            weights = jnp.concatenate([laid(row, column), laid(row, column + 1)], axis=1)
            response = jnp.dot(stack[...], weights, preferred_element_type=jnp.float32)
            active = jnp.maximum(response, 0.0)
            for half in range(2):
                for p in range(2):
                    inside = [m for m in range(windows) if (2 * m + row >= 7) == (p == 1)]
                    part = sum(active[m * count:(m + 1) * count, 128 * half:128 * half + 128] for m in inside)
                    place = 2 * p + (column + half >= 7)
                    total[place] = part if total[place] is None else total[place] + part
    pooled = jnp.concatenate(total, axis=1) * (1.0 / 49.0)
    order = pooled.shape[1]
    source = lax.broadcasted_iota(jnp.int32, (order, order), 0)
    target = lax.broadcasted_iota(jnp.int32, (order, order), 1)
    moved = (target == 4 * (source % 128) + source // 128).astype(jnp.float32).astype(jnp.bfloat16)
    stacked = jnp.concatenate([piece.astype(jnp.bfloat16) for piece in pieces(pooled)], axis=0)
    placed = jnp.dot(stacked, moved, preferred_element_type=jnp.float32)
    block[:count, :] = placed[:count] + placed[count:2 * count] + placed[2 * count:]
    block[count:, :] = jnp.zeros((8, order), jnp.float32)
    block[count:count + 1, :count] = labels[...].astype(jnp.float32)


def features_block(images, labels, seeds):
    count, pixels = images.shape
    order = 4 * seeds.shape[0]
    windows = (pixels // 3 - 256) // 128 + 1
    vmem = pl.BlockSpec(memory_space=pltpu.VMEM)
    return pl.pallas_call(
        features_kernel,
        out_shape=jax.ShapeDtypeStruct((count + 8, order), jnp.float32),
        in_specs=[vmem] * 3,
        out_specs=vmem,
        scratch_shapes=[
            pltpu.VMEM((windows * count, 768), jnp.bfloat16),
            pltpu.VMEM((8, 96 + 768, 128), jnp.float32),
            pltpu.VMEM((8, 96 + 768, 128), jnp.bfloat16),
        ],
        compiler_params=pltpu.CompilerParams(vmem_limit_bytes=24 * 1024 * 1024),
        name="features",
    )(images, seeds[None, :], labels[None, :])


def visit(here, step, length):
    ends = jnp.minimum(here, length - 1 - here)
    near = step <= 2 * ends
    away = jnp.where(near, (step + 1) // 2, step - ends)
    below = jnp.where(near, step % 2 == 1, here > length - 1 - here)
    return jnp.where(below, here - away, here + away)


def piece_cuts(rows, deep):
    early = 8 * round(rows / (16 * (deep - 1)))
    middle = early + 8 * ((rows - early) // 16)
    return 0, early, middle, rows


def gather_kernel(span, ridge, block, gram, sums, held, local_sem, send_sem, recv_sem):
    wide, deep = span
    x, z, c = lax.axis_index("sub"), lax.axis_index("img"), lax.axis_index("cls")
    across, other = wide - 1 - x, 1 - c
    count, order = block.shape[0] - 8, block.shape[1]
    classes = sums.shape[0]
    has_up, has_down = z < deep - 1, z > 0
    targets = ({"img": z + 1}, {"img": z - 1}, {"sub": across}, {"cls": other})

    barrier = pltpu.get_barrier_semaphore()
    for exists, target in zip((has_up, has_down, True, True), targets):
        if exists is True:
            pl.semaphore_signal(barrier, inc=1, device_id=target, device_id_type=MESH)
        else:
            @pl.when(exists)
            def _():
                pl.semaphore_signal(barrier, inc=1, device_id=target, device_id_type=MESH)
    own = pltpu.make_async_copy(block, held.at[x, z, c], local_sem.at[0])
    own.start()
    gram[...] = jnp.zeros_like(gram)
    sums[...] = jnp.zeros_like(sums)
    pl.semaphore_wait(barrier, 2 + has_up.astype(jnp.int32) + has_down.astype(jnp.int32))
    own.wait()

    cuts = piece_cuts(block.shape[0], deep)

    def copy(way, i, j, k, piece):
        slot = held.at[i, j, k, pl.ds(cuts[piece], cuts[piece + 1] - cuts[piece])]
        return pltpu.make_async_remote_copy(
            src_ref=slot, dst_ref=slot, send_sem=send_sem.at[way, i, j, piece], recv_sem=recv_sem.at[i, j, k, piece],
            device_id=targets[way], device_id_type=MESH)

    def pass_along(i, j, piece):
        @pl.when(jnp.logical_and(j <= z, has_up))
        def _():
            copy(0, i, j, c, piece).start()

        @pl.when(jnp.logical_and(j >= z, has_down))
        def _():
            copy(1, i, j, c, piece).start()

    def accumulate(i, j):
        both = jnp.concatenate([held[i, j, 0, :count, :], held[i, j, 1, :count, :]], axis=0)
        high = both.astype(jnp.bfloat16)
        low = (both - high.astype(jnp.float32)).astype(jnp.bfloat16)
        high_t, low_t = high.T, low.T
        label = jnp.concatenate([held[i, j, 0, count:count + 1, :count], held[i, j, 1, count:count + 1, :count]], axis=1)
        index = lax.broadcasted_iota(jnp.int32, (classes, 2 * count), 0) + c * (CLASSES // 2)
        onehot = (index == label.astype(jnp.int32)).astype(jnp.float32).astype(jnp.bfloat16)
        for base in range(0, order, PANEL):
            rows = slice(base, base + PANEL)
            total = jnp.dot(high_t[rows], high[:, base:], preferred_element_type=jnp.float32)
            total += jnp.dot(high_t[rows], low[:, base:], preferred_element_type=jnp.float32)
            total += jnp.dot(low_t[rows], high[:, base:], preferred_element_type=jnp.float32)
            total += jnp.dot(low_t[rows], low[:, base:], preferred_element_type=jnp.float32)
            gram[rows, base:] += total
        marked = jnp.dot(onehot, high, preferred_element_type=jnp.float32)
        marked += jnp.dot(onehot, low, preferred_element_type=jnp.float32)
        sums[...] += marked

    @pl.loop(0, deep + 2)
    def _(step):
        now = visit(z, jnp.minimum(step, deep - 1), deep)
        last = visit(z, jnp.clip(step - 1, 0, deep - 1), deep)
        older = visit(z, jnp.clip(step - 2, 0, deep - 1), deep)
        arriving = step < deep
        crossing = jnp.logical_and(step >= 1, step <= deep)

        @pl.when(crossing)
        def _():
            copy(3, across, last, c, 0).wait_recv()
            pass_along(across, last, 0)
            copy(3, across, last, c, 0).start()

        def line(piece):
            @pl.when(arriving)
            def _():
                @pl.when(step > 0)
                def _():
                    copy(3, x, now, c, piece).wait_recv()

                pass_along(x, now, piece)

                @pl.when(jnp.logical_or(step == 0, piece > 0))
                def _():
                    copy(2, x, now, c, piece).start()

                copy(3, x, now, c, piece).start()

        def cross(piece):
            @pl.when(crossing)
            def _():
                copy(3, across, last, c, piece).wait_recv()
                copy(3, across, last, c, piece).start()

        def add(i, j):
            for piece in range(3):
                copy(3, i, j, other, piece).wait_recv()
            accumulate(i, j)

        line(0)
        line(1)

        @pl.when(crossing)
        def _():
            add(x, last)

        line(2)
        cross(1)

        @pl.when(step >= 2)
        def _():
            add(across, older)

        cross(2)

    for base in range(0, order, PANEL):
        rows = slice(base, base + PANEL)
        lane = lax.broadcasted_iota(jnp.int32, (PANEL, PANEL), 1)
        down = lax.broadcasted_iota(jnp.int32, (PANEL, PANEL), 0)
        gram[rows, rows] += jnp.where(lane == down, ridge, 0.0)

    @pl.loop(0, deep)
    def _(j):
        for piece in range(3):
            for i in (x, across):
                if piece == 0 or i is x:
                    @pl.when(jnp.logical_and(j <= z, has_up))
                    def _():
                        copy(0, i, j, c, piece).wait_send()

                    @pl.when(jnp.logical_and(j >= z, has_down))
                    def _():
                        copy(1, i, j, c, piece).wait_send()

                copy(3, i, j, c, piece).wait_send()

            @pl.when(jnp.logical_or(j == z, piece > 0))
            def _():
                copy(2, x, j, c, piece).wait_send()


def gathered_sums(block, span, ridge, classes):
    order = block.shape[1]
    vmem = pl.BlockSpec(memory_space=pltpu.VMEM)
    return pl.pallas_call(
        lambda *refs: gather_kernel(span, ridge, *refs),
        out_shape=(jax.ShapeDtypeStruct((order, order), jnp.float32), jax.ShapeDtypeStruct((classes, order), jnp.float32)),
        in_specs=[vmem],
        out_specs=(vmem, vmem),
        scratch_shapes=[
            pltpu.VMEM((*span, 2, *block.shape), jnp.float32),
            pltpu.SemaphoreType.DMA((1,)),
            pltpu.SemaphoreType.DMA((4, *span, 3)),
            pltpu.SemaphoreType.DMA((*span, 2, 3)),
        ],
        compiler_params=pltpu.CompilerParams(collective_id=0, has_side_effects=True, vmem_limit_bytes=32 * 1024 * 1024),
        name="gather_sums",
    )(block)


def reduced_sums(feats, labels, ridge):
    index = jnp.arange(CLASSES, dtype=jnp.int32)
    onehot = (labels[:, None] == index[None, :]).astype(jnp.float32)
    over = (((0,), (0,)), ((), ()))
    gram = lax.dot_general(feats, feats, over, precision=HIGHEST, preferred_element_type=jnp.float32)
    sums = lax.dot_general(feats, onehot, over, precision=HIGHEST, preferred_element_type=jnp.float32)
    gram = lax.psum_scatter(gram, "cls", scatter_dimension=1, tiled=True)
    sums = lax.psum_scatter(sums, "cls", scatter_dimension=1, tiled=True)
    gram, sums = lax.psum((gram, sums), ("img", "sub"))
    gram = lax.all_gather(gram, "cls", axis=1, tiled=True)
    return gram + ridge * jnp.eye(gram.shape[0], dtype=jnp.float32), sums.T


def shards(images, labels, seeds):
    count = images.shape[0]
    block = features_block(images, labels, seeds)
    order = block.shape[1]
    span = (lax.axis_size("sub"), lax.axis_size("img"))
    pair = lax.axis_size("cls")
    ridge = RIDGE * count * span[0] * span[1] * pair
    held_bytes = span[0] * span[1] * pair * block.size * 4
    if span[0] == 2 and span[1] > 1 and pair == 2 and count == 128 and held_bytes <= GATHER_LIMIT:
        gram, sums = gathered_sums(block, span, ridge, CLASSES // pair)
    else:
        gram, sums = reduced_sums(block[:count], labels, ridge)
    rfactor, projections = factor(gram, sums)
    return rfactor, projections.T


def solution(mesh):
    placed = (P(("grp", "img", "sub", "cls"), None), P(("grp", "img", "sub", "cls")), P())
    return jax.shard_map(
        shards,
        mesh=mesh,
        in_specs=placed,
        out_specs=(P("grp", None), P("grp", "cls")),
        check_vma=False,
    )
```

profile of v0, /device:TPU:1, one launch (start us, length us, event | category | flops | bytes accessed | tf_op | source)
XLA Modules:
  0.0 57.8 jit_solution(11843137147721911834)
XLA Ops:
  0.6 0.0 copy-start.1
  0.6 0.0 copy-start.2
  0.6 0.6 %copy-done.1 = s32[128]{0:T(128)S(1)} copy-done((s32[128]{0:T(128)S(1)}, s32[128]{0:T(128)}, u32[]{:S(2)}) %copy-start.1) | copy-done | bytes 536
  1.3 0.0 copy-done.2
  1.3 0.0 copy-start
  1.3 1.1 %copy-done = bf16[128,3072]{1,0:T(8,128)(2,1)S(1)} copy-done((bf16[128,3072]{1,0:T(8,128)(2,1)S(1)}, bf16[128,3072]{1,0:T(8,128)(2,1)}, u32[]{:S(2)}) %copy-start) | copy-done | bytes 786456
  2.4 5.6 %features.1.refs_0_ = f32[136,512]{1,0:T(8,128)S(1)} custom-call(bf16[128,3072]{1,0:T(8,128)(2,1)S(1)} %copy-done, s32[1,128]{1,0:T(1,128)S(1)} %bitcast.3, s32[1,128]{1,0:T(1,128)S(1)} %bitcast.4), custom_call_target="tpu_custom_call" | custom-call | tf_op jit(solution)/shard_map/features/pallas_call | solution.py:199
  8.0 34.0 %gather_sums.1 = (f32[512,512]{1,0:T(8,128)S(1)}, f32[500,512]{1,0:T(8,128)S(1)}) custom-call(f32[136,512]{1,0:T(8,128)S(1)} %features.1.refs_0_), custom_call_target="tpu_custom_call" | custom-call | tf_op jit(solution)/shard_map/gather_sums/pallas_call | solution.py:373
  42.1 15.6 %factor.1 = (f32[512,512]{1,0:T(8,128)}, f32[500,512]{1,0:T(8,128)}) custom-call(f32[512,512]{1,0:T(8,128)S(1)} %get-tuple-element.6.gram, f32[500,512]{1,0:T(8,128)S(1)} %get-tuple-element.7.sums), custom_call_target="tpu_custom_call" | custom-call | tf_op jit(solution)/shard_map/factor/pallas_call | solution.py:125
Async XLA Ops:
  0.6 0.7 %copy-start.1 = (s32[128]{0:T(128)S(1)}, s32[128]{0:T(128)}, u32[]{:S(2)}) copy-start(s32[128]{0:T(128)} %param.5) | copy-start | bytes 1540
  0.6 0.7 %copy-start.2 = (s32[128]{0:T(128)S(1)}, s32[128]{0:T(128)}, u32[]{:S(2)}) copy-start(s32[128]{0:T(128)} %param.4) | copy-start | bytes 1540
  1.3 1.1 %copy-start = (bf16[128,3072]{1,0:T(8,128)(2,1)S(1)}, bf16[128,3072]{1,0:T(8,128)(2,1)}, u32[]{:S(2)}) copy-start(bf16[128,3072]{1,0:T(8,128)(2,1)} %images.1) | copy-start | bytes 2359300
where the time goes:
time: 58 us; the launch traced here: 57.8 us
  Pallas kernels  55.2 us (95%)
  local copies, waits for them, and re-layouts  1.79 us (3%)
  between operations  0.82 us (1%)
    pallas_call x1, Pallas kernels, gathered_sums(): pl.pallas_call(lambda *refs: gather_kernel(span, ridge, *refs), out_shape...  34 us
    pallas_call x1, Pallas kernels, factor(): pl.pallas_call(factor_kernel, out_shape=(jax.ShapeDtypeStruct(gram.shape,...  15.6 us
    pallas_call x1, Pallas kernels, features_block(): pl.pallas_call(features_kernel, out_shape=jax.ShapeDtypeStruct((count + 8...  5.59 us
    unnamed x6, local copies, waits for them, and re-layouts  1.79 us

commit v1 on v0

v1 whole, which is shorter than its diff:
```python
import math

import jax
import jax.numpy as jnp
from jax import lax
from jax.experimental import pallas as pl
from jax.experimental.pallas import tpu as pltpu
from jax.sharding import PartitionSpec as P

CLASSES = 1000
RIDGE = 0.001
PANEL = 128
STRIP = 32
BAND = 128
GATHER_LIMIT = 16 * 1024 * 1024
HIGHEST = lax.Precision.HIGHEST
MESH = pl.DeviceIdType.MESH


def pieces(value):
    first = value.astype(jnp.bfloat16).astype(jnp.float32)
    rest = value - first
    second = rest.astype(jnp.bfloat16).astype(jnp.float32)
    return first, second, rest - second


def product(left, right, left_dim, right_dim):
    l1, l2, l3 = pieces(left)
    r1, r2, r3 = pieces(right)
    lefts = jnp.concatenate([l1, l1, l2, l1, l3, l2], axis=left_dim).astype(jnp.bfloat16)
    rights = jnp.concatenate([r1, r2, r1, r3, r1, r2], axis=right_dim).astype(jnp.bfloat16)
    over = (((left_dim,), (right_dim,)), ((), ()))
    return lax.dot_general(lefts, rights, over, preferred_element_type=jnp.float32)


def factor_block(work, hooks=()):
    tiles = STRIP // 8
    sub = lax.broadcasted_iota(jnp.int32, (8, PANEL), 0)

    def spread(tile, row):
        return jnp.broadcast_to(tile[row:row + 1, :], (8, tile.shape[1]))

    def double(tile):
        return jnp.concatenate([tile, tile], axis=1)

    for base in range(0, PANEL, STRIP):
        rows = [work[base + 8 * h:base + 8 * h + 8, :] for h in range(tiles)]
        cols = {}
        for j in range(STRIP):
            for h in range(j // 8, tiles):
                cols[j, h] = jnp.broadcast_to(rows[h][:, base + j:base + j + 1], (8, PANEL))
        scale = [None] * tiles
        for k in range(0, STRIP, 2):
            own, row = divmod(k, 8)
            one = spread(cols[k, own], row)
            cross = spread(cols[k, own], row + 1)
            two = spread(cols[k + 1, own], row + 1)
            det = one * two - cross * cross
            one_inverse = 1.0 / one
            two_inverse = one / det
            ratio = cross * one_inverse
            paired = jnp.where(sub > row, det * one_inverse, one)
            scale[own] = paired if scale[own] is None else jnp.where(sub >= row, paired, scale[own])
            first, second, rest = {}, {}, {}
            for h in range(own, tiles):
                first[h] = cols[k, h] * one_inverse
                rest[h] = cols[k + 1, h] - first[h] * cross
                second[h] = rest[h] * two_inverse
                if h == own:
                    first[h] = jnp.where(sub > row, first[h], 0.0)
                    second[h] = jnp.where(sub > row + 1, second[h], 0.0)
            for j in range(k + 2, STRIP):
                peer, place = divmod(j, 8)
                entry = spread(cols[k, peer], place)
                other = spread(rest[peer], place)
                for h in range(peer, tiles):
                    cols[j, h] = cols[j, h] - first[h] * entry - second[h] * other
            line = spread(rows[own], row)
            next_line = spread(rows[own], row + 1) - double(ratio) * line
            for h in range(own, tiles):
                rows[h] = rows[h] - double(first[h]) * line - double(second[h]) * next_line
        for h in range(tiles):
            rows[h] = rows[h] * double(lax.rsqrt(scale[h]))
            work[base + 8 * h:base + 8 * h + 8, :] = rows[h]
        for hook in hooks[base // STRIP:base // STRIP + 1]:
            hook()
        low = base + STRIP
        if low < PANEL:
            strip = jnp.concatenate(rows, axis=0)
            work[low:, :] = work[low:, :] - product(strip[:, low:PANEL], strip, 0, 0)


def factor_kernel(gram, sums, rfactor, projections, square, solved, work, sems):
    order = gram.shape[0]
    lane = lax.broadcasted_iota(jnp.int32, (PANEL, PANEL), 1)
    down = lax.broadcasted_iota(jnp.int32, (PANEL, PANEL), 0)
    square[...] = gram[...]
    solved[...] = sums[...]
    copies = []
    for number, base in enumerate(range(0, order, PANEL)):
        end = base + PANEL
        work[:, :PANEL] = square[base:end, base:end]
        work[:, PANEL:] = (lane == down).astype(jnp.float32)
        factor_block(work)
        inverse = work[:, PANEL:]
        square[base:end, base:end] = jnp.where(lane >= down, work[:, :PANEL], 0.0)
        if base:
            square[base:end, :base] = jnp.zeros((PANEL, base), jnp.float32)
        answer = product(solved[:, base:end], inverse, 1, 1)
        solved[:, base:end] = answer
        if end < order:
            panel = product(inverse, square[base:end, end:], 1, 0)
            square[base:end, end:] = panel
            for top in range(end, order, PANEL):
                square[top:top + PANEL, top:] = square[top:top + PANEL, top:] - product(panel[:, top - end:top - end + PANEL], panel[:, top - end:], 0, 0)
            solved[:, end:] = solved[:, end:] - product(answer, panel, 1, 0)
        copies.append(pltpu.make_async_copy(square.at[pl.ds(base, PANEL)], rfactor.at[pl.ds(base, PANEL)], sems.at[0, number]))
        copies.append(pltpu.make_async_copy(solved.at[:, pl.ds(base, PANEL)], projections.at[:, pl.ds(base, PANEL)], sems.at[1, number]))
        copies[-2].start()
        copies[-1].start()
    for copy in copies:
        copy.wait()


def factor(gram, sums):
    vmem = pl.BlockSpec(memory_space=pltpu.VMEM)
    order = gram.shape[0]
    return pl.pallas_call(
        factor_kernel,
        out_shape=(jax.ShapeDtypeStruct(gram.shape, jnp.float32), jax.ShapeDtypeStruct(sums.shape, jnp.float32)),
        in_specs=[vmem, vmem],
        out_specs=(pl.BlockSpec(memory_space=pl.ANY),) * 2,
        scratch_shapes=[
            pltpu.VMEM(gram.shape, jnp.float32),
            pltpu.VMEM(sums.shape, jnp.float32),
            pltpu.VMEM((PANEL, 2 * PANEL), jnp.float32),
            pltpu.SemaphoreType.DMA((2, order // PANEL)),
        ],
        compiler_params=pltpu.CompilerParams(vmem_limit_bytes=16 * 1024 * 1024),
        name="factor",
    )(gram, sums)


def make_weights(seeds, weights):
    down = lax.broadcasted_iota(jnp.int32, (8, 128), 0)
    seed = jnp.broadcast_to(seeds[...], (8, 128))
    tiles = {}
    for c in range(3):
        for a in range(6):
            index = 36 * c + 6 * a + down
            first = lax.rem(seed * 7919 + index * 104729, 46337)
            second = lax.rem(first * first + seed, 46337)
            values = (second.astype(jnp.float32) / 46337.0 - 0.5) * math.sqrt(12.0 / 108.0)
            values = jnp.where(down < 6, values, 0.0)
            tiles[c, a, 0] = values
            tiles[c, a, 1] = pltpu.roll(values, 2, 0)
    none = jnp.zeros((8, 128), jnp.float32)
    for g in range(4):
        for place in range(4):
            below, right = divmod(place, 2)
            column = []
            for spot in range(32):
                half, position = divmod(spot, 16)
                c = (position - g) % 4
                a = 4 * half + ((position - c) % 16) // 4 - 2 * below
                column.append(tiles[c, a, right] if c < 3 and 0 <= a < 6 else none)
            weights[g, :, 128 * place:128 * place + 128] = jnp.concatenate(column, axis=0).astype(jnp.bfloat16)


def make_windows(images, windows):
    count, pixels = images.shape
    plane = pixels // 3
    group = lax.rem(lax.broadcasted_iota(jnp.int32, (count, BAND), 1) // 8, 4)
    for b in range(plane // BAND):
        units = [images[:, plane * c + BAND * b:plane * c + BAND * b + BAND] for c in range(3)]
        for off in range(2):
            turned = [pltpu.roll(unit, (8 * c - 4 * off) % BAND, 1) if 8 * c - 4 * off else unit for c, unit in enumerate(units)]
            for g in range(4 - off):
                mixed = jnp.where(group == (g + 1) % 4, turned[1], turned[2])
                mixed = jnp.where(group == g, turned[0], mixed)
                windows[2 * g + off, b * count:(b + 1) * count, :] = mixed


def pooled_features(count, weights, windows):
    bands = windows.shape[1] // count
    steps = bands - 1
    total = [None] * 4
    for w in range(windows.shape[0]):
        g = w // 2
        taken = jnp.concatenate([windows[w, :steps * count, :], windows[w, count:, :]], axis=1)
        for row in range(2):
            response = jnp.dot(taken, weights[g, :, 256 * row:256 * row + 256], preferred_element_type=jnp.float32)
            active = jnp.maximum(response, 0.0)
            for half in range(2):
                for p in range(2):
                    inside = [m for m in range(steps) if (2 * m + row >= 7) == (p == 1)]
                    part = sum(active[m * count:(m + 1) * count, 128 * half:128 * half + 128] for m in inside)
                    place = 2 * p + (2 * w + half >= 7)
                    total[place] = part if total[place] is None else total[place] + part
    return jnp.concatenate(total, axis=1) * (1.0 / 49.0)


def make_order(moved):
    order = moved.shape[0]
    source = lax.broadcasted_iota(jnp.int32, (order, order), 0)
    target = lax.broadcasted_iota(jnp.int32, (order, order), 1)
    moved[...] = (target == 4 * (source % 128) + source // 128).astype(jnp.float32).astype(jnp.bfloat16)


def placed_features(pooled, moved):
    count = pooled.shape[0]
    stacked = jnp.concatenate([piece.astype(jnp.bfloat16) for piece in pieces(pooled)], axis=0)
    placed = jnp.dot(stacked, moved[...], preferred_element_type=jnp.float32)
    return placed[:count] + placed[count:2 * count] + placed[2 * count:]


def feature_scratch(count, plane):
    return [
        pltpu.VMEM((4, 256, 512), jnp.bfloat16),
        pltpu.VMEM((7, plane // BAND * count, BAND), jnp.bfloat16),
        pltpu.VMEM((512, 512), jnp.bfloat16),
    ]


def features_kernel(images, seeds, block, weights, windows, moved):
    make_weights(seeds, weights)
    make_order(moved)
    make_windows(images, windows)
    block[...] = placed_features(pooled_features(images.shape[0], weights, windows), moved)


def features_block(images, seeds):
    count, pixels = images.shape
    vmem = pl.BlockSpec(memory_space=pltpu.VMEM)
    return pl.pallas_call(
        features_kernel,
        out_shape=jax.ShapeDtypeStruct((count, 4 * seeds.shape[0]), jnp.float32),
        in_specs=[vmem] * 2,
        out_specs=vmem,
        scratch_shapes=feature_scratch(count, pixels // 3),
        compiler_params=pltpu.CompilerParams(vmem_limit_bytes=24 * 1024 * 1024),
        name="features",
    )(images, seeds[None, :])


def visit(here, step, length):
    ends = jnp.minimum(here, length - 1 - here)
    near = step <= 2 * ends
    away = jnp.where(near, (step + 1) // 2, step - ends)
    below = jnp.where(near, step % 2 == 1, here > length - 1 - here)
    return jnp.where(below, here - away, here + away)


def panel_kernel(span, ridge, images, seeds, labels, square, solved, picture, seed_row, label_row, weights, windows, moved,
                 held, left_high, left_low, onehot, gram, sums, inverses, work, local_sem, send_sem, recv_sem):
    wide, deep = span
    x, z, c = lax.axis_index("sub"), lax.axis_index("img"), lax.axis_index("cls")
    across, other = wide - 1 - x, 1 - c
    count = picture.shape[0]
    order, classes = square.shape[0], solved.shape[0]
    stages = order // PANEL
    targets = [{"img": lax.rem(z + d, deep)} for d in range(1, deep)] + [{"sub": across}, {"cls": other}]
    over_x, over_c = deep - 1, deep

    loads = [pltpu.make_async_copy(seeds, seed_row, local_sem.at[0]),
             pltpu.make_async_copy(images, picture, local_sem.at[1]),
             pltpu.make_async_copy(labels, label_row, local_sem.at[2])]
    for load in loads:
        load.start()
    barrier = pltpu.get_barrier_semaphore()
    for target in targets:
        pl.semaphore_signal(barrier, inc=1, device_id=target, device_id_type=MESH)
    make_order(moved)
    square[...] = jnp.zeros_like(square)
    gram[...] = jnp.zeros_like(gram)
    sums[...] = jnp.zeros_like(sums)
    lane = lax.broadcasted_iota(jnp.int32, (PANEL, PANEL), 1)
    down = lax.broadcasted_iota(jnp.int32, (PANEL, PANEL), 0)
    for load in loads:
        load.wait()
    make_weights(seed_row, weights)
    make_windows(picture, windows)
    placed = placed_features(pooled_features(count, weights, windows), moved)
    for q in range(stages):
        held[x, z, c, 8 + PANEL * q:8 + PANEL * q + count, :] = placed[:, PANEL * q:PANEL * q + PANEL]
    held[x, z, c, 0:8, :] = jnp.broadcast_to(label_row[...].astype(jnp.float32), (8, count))
    pl.semaphore_wait(barrier, len(targets))

    def copy(way, i, j, k, q):
        low = 0 if q == 0 else 8 + PANEL * q
        slot = held.at[i, j, k, pl.ds(low, 8 + PANEL * q + count - low)]
        return pltpu.make_async_remote_copy(
            src_ref=slot, dst_ref=slot, send_sem=send_sem.at[way, i, j, q], recv_sem=recv_sem.at[i, j, k, q],
            device_id=targets[way], device_id_type=MESH)

    def start_own(q):
        for way in list(range(deep - 1)) + [over_c]:
            copy(way, x, z, c, q).start()

    def relay(q, d):
        j = visit(z, d, deep)
        copy(over_x, x, j, c, q).wait_recv()
        copy(over_x, x, j, c, q).start()
        copy(over_c, x, j, c, q).start()

    def cross(q, d):
        j = visit(z, d, deep)
        copy(over_x, across, j, c, q).wait_recv()
        copy(over_c, across, j, c, q).start()

    def accumulate(q, i, j):
        chunk = i * deep + j
        low = 8 + PANEL * q
        copy(over_c, i, j, other, q).wait_recv()
        both = jnp.concatenate([held[i, j, 0, low:low + count, :], held[i, j, 1, low:low + count, :]], axis=0)
        high = both.astype(jnp.bfloat16)
        rest = (both - high.astype(jnp.float32)).astype(jnp.bfloat16)
        left_high[chunk, PANEL * q:PANEL * q + PANEL, :] = high.T
        left_low[chunk, PANEL * q:PANEL * q + PANEL, :] = rest.T
        if q == 0:
            label = jnp.concatenate([held[i, j, 0, 0:1, :], held[i, j, 1, 0:1, :]], axis=1)
            index = lax.broadcasted_iota(jnp.int32, (classes, 2 * count), 0) + c * classes
            onehot[chunk] = (index == label.astype(jnp.int32)).astype(jnp.float32).astype(jnp.bfloat16)
        pair = jnp.concatenate([high, rest], axis=1)
        end = PANEL * q + PANEL
        top = jnp.dot(left_high[chunk, :end, :], pair, preferred_element_type=jnp.float32)
        bottom = jnp.dot(left_low[chunk, :end, :], pair, preferred_element_type=jnp.float32)
        gram[:end, PANEL * q:end] += (top[:, :PANEL] + top[:, PANEL:]) + (bottom[:, :PANEL] + bottom[:, PANEL:])
        marked = jnp.dot(onehot[chunk], pair, preferred_element_type=jnp.float32)
        sums[:, PANEL * q:end] += marked[:, :PANEL] + marked[:, PANEL:]

    copy(over_x, x, z, c, 0).start()
    for q in range(stages):
        start_own(q)

    pending = []
    for q in range(stages):
        for act in pending:
            act()
        if q == 0:
            for d in range(1, deep):
                relay(0, d)
            copy(over_x, x, z, c, 1).start()
            for d in range(deep):
                cross(0, d)

        @pl.loop(0, deep)
        def _(d):
            j = visit(z, d, deep)
            accumulate(q, x, j)
            accumulate(q, across, j)

        base, end = PANEL * q, PANEL * q + PANEL
        for i in range(q):
            rows = slice(PANEL * i, PANEL * i + PANEL)
            value = gram[rows, base:end]
            if i:
                value = value - product(square[:PANEL * i, rows], square[:PANEL * i, base:end], 0, 0)
            square[rows, base:end] = product(inverses[i], value, 1, 0)
        value = gram[base:end, base:end] + jnp.where(lane == down, ridge, 0.0)
        tail = sums[:, base:end]
        if q:
            value = value - product(square[:base, base:end], square[:base, base:end], 0, 0)
            tail = tail - product(solved[:, :base], square[:base, base:end], 1, 0)
        if q == stages - 1:
            square[base:end, base:end] = value
            solved[:, base:end] = tail
            continue
        work[:, :PANEL] = value
        work[:, PANEL:] = (lane == down).astype(jnp.float32)
        acts = []
        for d in range(deep):
            if d:
                acts.append(lambda q=q, d=d: relay(q + 1, d))
            acts.append(lambda q=q, d=d: cross(q + 1, d))
        if q + 2 < stages:
            acts.insert(deep, lambda q=q: copy(over_x, x, z, c, q + 2).start())
        strips = PANEL // STRIP

        def hook(part):
            for act in part:
                act()

        size = -(-len(acts) // strips)
        parts = [acts[n * size:n * size + size] for n in range(strips)]
        pending = []
        factor_block(work, [lambda part=part: hook(part) for part in parts])
        inverses[q] = work[:, PANEL:]
        square[base:end, base:end] = jnp.where(lane >= down, work[:, :PANEL], 0.0)
        solved[:, base:end] = product(tail, work[:, PANEL:], 1, 1)

    for q in range(stages):
        for way in range(deep - 1):
            copy(way, x, z, c, q).wait_send()

        @pl.loop(0, deep)
        def _(j):
            copy(over_x, x, j, c, q).wait_send()
            copy(over_c, x, j, c, q).wait_send()
            copy(over_c, across, j, c, q).wait_send()


def panel(images, seeds, labels, span, ridge, classes):
    count, pixels = images.shape
    order = 4 * seeds.shape[0]
    wide, deep = span
    stages = order // PANEL
    vmem, whole = pl.BlockSpec(memory_space=pltpu.VMEM), pl.BlockSpec(memory_space=pl.ANY)
    return pl.pallas_call(
        lambda *refs: panel_kernel(span, ridge, *refs),
        out_shape=(jax.ShapeDtypeStruct((order, order), jnp.float32), jax.ShapeDtypeStruct((classes, order), jnp.float32)),
        in_specs=[whole] * 3,
        out_specs=(vmem, vmem),
        scratch_shapes=[
            pltpu.VMEM((count, pixels), jnp.bfloat16),
            pltpu.VMEM((1, seeds.shape[0]), jnp.int32),
            pltpu.VMEM((1, count), jnp.int32),
            *feature_scratch(count, pixels // 3),
            pltpu.VMEM((wide, deep, 2, 8 + stages * count, PANEL), jnp.float32),
            pltpu.VMEM((wide * deep, order, 2 * count), jnp.bfloat16),
            pltpu.VMEM((wide * deep, order, 2 * count), jnp.bfloat16),
            pltpu.VMEM((wide * deep, classes, 2 * count), jnp.bfloat16),
            pltpu.VMEM((order, order), jnp.float32),
            pltpu.VMEM((classes, order), jnp.float32),
            pltpu.VMEM((stages, PANEL, PANEL), jnp.float32),
            pltpu.VMEM((PANEL, 2 * PANEL), jnp.float32),
            pltpu.SemaphoreType.DMA((3,)),
            pltpu.SemaphoreType.DMA((deep + 1, wide, deep, stages)),
            pltpu.SemaphoreType.DMA((wide, deep, 2, stages)),
        ],
        compiler_params=pltpu.CompilerParams(collective_id=0, has_side_effects=True, vmem_limit_bytes=40 * 1024 * 1024),
        name="panel",
    )(images, seeds[None, :], labels[None, :])


def finish_kernel(square, solved, rfactor, projections, block, answer, work, sems):
    order = square.shape[0]
    base = order - PANEL
    lane = lax.broadcasted_iota(jnp.int32, (PANEL, PANEL), 1)
    down = lax.broadcasted_iota(jnp.int32, (PANEL, PANEL), 0)
    copies = [pltpu.make_async_copy(square.at[pl.ds(0, base)], rfactor.at[pl.ds(0, base)], sems.at[0]),
              pltpu.make_async_copy(solved.at[:, pl.ds(0, base)], projections.at[:, pl.ds(0, base)], sems.at[1]),
              pltpu.make_async_copy(block, rfactor.at[pl.ds(base, PANEL)], sems.at[2]),
              pltpu.make_async_copy(answer, projections.at[:, pl.ds(base, PANEL)], sems.at[3])]
    copies[0].start()
    copies[1].start()
    work[:, :PANEL] = square[base:, base:]
    work[:, PANEL:] = (lane == down).astype(jnp.float32)
    factor_block(work)
    block[...] = jnp.zeros_like(block)
    block[:, base:] = jnp.where(lane >= down, work[:, :PANEL], 0.0)
    copies[2].start()
    answer[...] = product(solved[:, base:], work[:, PANEL:], 1, 1)
    copies[3].start()
    for copy in copies:
        copy.wait()


def finish(square, solved):
    vmem = pl.BlockSpec(memory_space=pltpu.VMEM)
    order = square.shape[0]
    return pl.pallas_call(
        finish_kernel,
        out_shape=(jax.ShapeDtypeStruct(square.shape, jnp.float32), jax.ShapeDtypeStruct(solved.shape, jnp.float32)),
        in_specs=[vmem, vmem],
        out_specs=(pl.BlockSpec(memory_space=pl.ANY),) * 2,
        scratch_shapes=[
            pltpu.VMEM((PANEL, order), jnp.float32),
            pltpu.VMEM((solved.shape[0], PANEL), jnp.float32),
            pltpu.VMEM((PANEL, 2 * PANEL), jnp.float32),
            pltpu.SemaphoreType.DMA((4,)),
        ],
        compiler_params=pltpu.CompilerParams(vmem_limit_bytes=16 * 1024 * 1024),
        name="finish",
    )(square, solved)


def reduced_sums(feats, labels, ridge):
    index = jnp.arange(CLASSES, dtype=jnp.int32)
    onehot = (labels[:, None] == index[None, :]).astype(jnp.float32)
    over = (((0,), (0,)), ((), ()))
    gram = lax.dot_general(feats, feats, over, precision=HIGHEST, preferred_element_type=jnp.float32)
    sums = lax.dot_general(feats, onehot, over, precision=HIGHEST, preferred_element_type=jnp.float32)
    gram = lax.psum_scatter(gram, "cls", scatter_dimension=1, tiled=True)
    sums = lax.psum_scatter(sums, "cls", scatter_dimension=1, tiled=True)
    gram, sums = lax.psum((gram, sums), ("img", "sub"))
    gram = lax.all_gather(gram, "cls", axis=1, tiled=True)
    return gram + ridge * jnp.eye(gram.shape[0], dtype=jnp.float32), sums.T


def shards(images, labels, seeds):
    count = images.shape[0]
    order = 4 * seeds.shape[0]
    span = (lax.axis_size("sub"), lax.axis_size("img"))
    pair = lax.axis_size("cls")
    ridge = RIDGE * count * span[0] * span[1] * pair
    held_bytes = span[0] * span[1] * pair * count * order * 4
    if span[0] == 2 and span[1] > 1 and pair == 2 and count == 128 and held_bytes <= GATHER_LIMIT:
        rfactor, projections = finish(*panel(images, seeds, labels, span, ridge, CLASSES // pair))
    else:
        gram, sums = reduced_sums(features_block(images, seeds), labels, ridge)
        rfactor, projections = factor(gram, sums)
    return rfactor, projections.T


def solution(mesh):
    placed = (P(("grp", "img", "sub", "cls"), None), P(("grp", "img", "sub", "cls")), P())
    return jax.shard_map(
        shards,
        mesh=mesh,
        in_specs=placed,
        out_specs=(P("grp", None), P("grp", "cls")),
        check_vma=False,
    )
```

time: 58 us -> 81.2 us (1.40)
  the two profiles are of different devices: /device:TPU:1 before, /device:TPU:10 now
where the time goes in v1:
time: 81.2 us; the launch traced here: 81 us
  Pallas kernels  78.4 us (97%)
  local copies, waits for them, and re-layouts  1.79 us (2%)
  between operations  0.82 us (1%)
    pallas_call x1, Pallas kernels, panel(): pl.pallas_call(lambda *refs: panel_kernel(span, ridge, *refs), out_shape=...  74.1 us
    pallas_call x1, Pallas kernels, finish(): pl.pallas_call(finish_kernel, out_shape=(jax.ShapeDtypeStruct(square.shap...  4.34 us
    unnamed x6, local copies, waits for them, and re-layouts  1.79 us

profile of v1, /device:TPU:10, one launch (start us, length us, event | category | flops | bytes accessed | tf_op | source)
XLA Modules:
  0.0 81.0 jit_solution(14471571475739170193)
XLA Ops:
  0.6 0.0 copy-start.1
  0.6 0.0 copy-start.2
  0.6 0.6 copy-done.1
  1.3 0.0 copy-done.2
  1.3 0.0 copy-start
  1.3 1.1 %copy-done = bf16[128,3072]{1,0:T(8,128)(2,1)S(1)} copy-done((bf16[128,3072]{1,0:T(8,128)(2,1)S(1)}, bf16[128,3072]{1,0:T(8,128)(2,1)}, u32[]{:S(2)}) %copy-start) | copy-done | bytes 786456
  2.4 74.1 %panel.1 = (f32[512,512]{1,0:T(8,128)S(1)}, f32[500,512]{1,0:T(8,128)S(1)}) custom-call(bf16[128,3072]{1,0:T(8,128)(2,1)S(1)} %copy-done, s32[1,128]{1,0:T(1,128)S(1)} %bitcast.3, s32[1,128]{1,0:T(1,128)S(1)} %bitcast.4), custom_call_target="tpu_custom_call" | custom-call | tf_op jit(solution)/shard_map/panel/pallas_call | solution.py:409
  76.5 4.3 %finish.1 = (f32[512,512]{1,0:T(8,128)}, f32[500,512]{1,0:T(8,128)}) custom-call(f32[512,512]{1,0:T(8,128)S(1)} %get-tuple-element.6.square, f32[500,512]{1,0:T(8,128)S(1)} %get-tuple-element.7.solved), custom_call_target="tpu_custom_call" | custom-call | tf_op jit(solution)/shard_map/finish/pallas_call | solution.py:462
Async XLA Ops:
  0.6 0.7 copy-start.1
  0.6 0.7 copy-start.2
  1.3 1.1 %copy-start = (bf16[128,3072]{1,0:T(8,128)(2,1)S(1)}, bf16[128,3072]{1,0:T(8,128)(2,1)}, u32[]{:S(2)}) copy-start(bf16[128,3072]{1,0:T(8,128)(2,1)} %refs_0_.1) | copy-start | bytes 2359300

commit v2 on v0

--- a/solution.py
+++ b/solution.py
@@ -11,6 +11,7 @@
 RIDGE = 0.001
 PANEL = 128
 STRIP = 32
+BAND = 128
 GATHER_LIMIT = 16 * 1024 * 1024
 HIGHEST = lax.Precision.HIGHEST
 MESH = pl.DeviceIdType.MESH
@@ -32,7 +33,7 @@
     return lax.dot_general(lefts, rights, over, preferred_element_type=jnp.float32)
 
 
-def factor_block(work):
+def factor_block(work, hooks=()):
     tiles = STRIP // 8
     sub = lax.broadcasted_iota(jnp.int32, (8, PANEL), 0)
 
@@ -81,6 +82,8 @@
         for h in range(tiles):
             rows[h] = rows[h] * double(lax.rsqrt(scale[h]))
             work[base + 8 * h:base + 8 * h + 8, :] = rows[h]
+        for hook in hooks[base // STRIP:base // STRIP + 1]:
+            hook()
         low = base + STRIP
         if low < PANEL:
             strip = jnp.concatenate(rows, axis=0)
@@ -138,14 +141,10 @@
     )(gram, sums)
 
 
-def features_kernel(images, seeds, labels, block, stack, spread, bank):
-    count, pixels = images.shape
-    plane = pixels // 3
-    windows = (plane - 256) // 128 + 1
-    lead = bank.shape[1] - 768
+def make_weights(seeds, weights):
     down = lax.broadcasted_iota(jnp.int32, (8, 128), 0)
     seed = jnp.broadcast_to(seeds[...], (8, 128))
-    spread[...] = jnp.zeros_like(spread)
+    tiles = {}
     for c in range(3):
         for a in range(6):
             index = 36 * c + 6 * a + down
@@ -153,59 +152,95 @@
             second = lax.rem(first * first + seed, 46337)
             values = (second.astype(jnp.float32) / 46337.0 - 0.5) * math.sqrt(12.0 / 108.0)
             values = jnp.where(down < 6, values, 0.0)
-            for shift in range(8):
-                top = lead + 256 * c + 32 * a + 2 * shift
-                spread[shift, top:top + 8, :] = values
-    for shift in range(8):
-        bank[shift] = spread[shift].astype(jnp.bfloat16)
-    for m in range(windows):
-        for c in range(3):
-            stack[m * count:(m + 1) * count, 256 * c:256 * c + 256] = images[:, plane * c + 128 * m:plane * c + 128 * m + 256]
-
-    def laid(row, column):
-        skip, shift = divmod(2 * column, 16)
-        top = lead - 64 * row - 16 * skip
-        return bank[shift // 2, top:top + 768, :]
-
+            tiles[c, a, 0] = values
+            tiles[c, a, 1] = pltpu.roll(values, 2, 0)
+    none = jnp.zeros((8, 128), jnp.float32)
+    for g in range(4):
+        for place in range(4):
+            below, right = divmod(place, 2)
+            column = []
+            for spot in range(32):
+                half, position = divmod(spot, 16)
+                c = (position - g) % 4
+                a = 4 * half + ((position - c) % 16) // 4 - 2 * below
+                column.append(tiles[c, a, right] if c < 3 and 0 <= a < 6 else none)
+            weights[g, :, 128 * place:128 * place + 128] = jnp.concatenate(column, axis=0).astype(jnp.bfloat16)
+
+
+def make_windows(images, windows):
+    count, pixels = images.shape
+    plane = pixels // 3
+    group = lax.rem(lax.broadcasted_iota(jnp.int32, (count, BAND), 1) // 8, 4)
+    for b in range(plane // BAND):
+        units = [images[:, plane * c + BAND * b:plane * c + BAND * b + BAND] for c in range(3)]
+        for off in range(2):
+            turned = [pltpu.roll(unit, (8 * c - 4 * off) % BAND, 1) if 8 * c - 4 * off else unit for c, unit in enumerate(units)]
+            for g in range(4 - off):
+                mixed = jnp.where(group == (g + 1) % 4, turned[1], turned[2])
+                mixed = jnp.where(group == g, turned[0], mixed)
+                windows[2 * g + off, b * count:(b + 1) * count, :] = mixed
+
+
+def pooled_features(count, weights, windows):
+    bands = windows.shape[1] // count
+    steps = bands - 1
     total = [None] * 4
-    for row in range(2):
-        for column in range(0, 14, 2):
-            weights = jnp.concatenate([laid(row, column), laid(row, column + 1)], axis=1)
-            response = jnp.dot(stack[...], weights, preferred_element_type=jnp.float32)
+    for w in range(windows.shape[0]):
+        g = w // 2
+        taken = jnp.concatenate([windows[w, :steps * count, :], windows[w, count:, :]], axis=1)
+        for row in range(2):
+            response = jnp.dot(taken, weights[g, :, 256 * row:256 * row + 256], preferred_element_type=jnp.float32)
             active = jnp.maximum(response, 0.0)
             for half in range(2):
                 for p in range(2):
-                    inside = [m for m in range(windows) if (2 * m + row >= 7) == (p == 1)]
+                    inside = [m for m in range(steps) if (2 * m + row >= 7) == (p == 1)]
                     part = sum(active[m * count:(m + 1) * count, 128 * half:128 * half + 128] for m in inside)
-                    place = 2 * p + (column + half >= 7)
+                    place = 2 * p + (2 * w + half >= 7)
                     total[place] = part if total[place] is None else total[place] + part
-    pooled = jnp.concatenate(total, axis=1) * (1.0 / 49.0)
-    order = pooled.shape[1]
+    return jnp.concatenate(total, axis=1) * (1.0 / 49.0)
+
+
+def make_order(moved):
+    order = moved.shape[0]
     source = lax.broadcasted_iota(jnp.int32, (order, order), 0)
     target = lax.broadcasted_iota(jnp.int32, (order, order), 1)
-    moved = (target == 4 * (source % 128) + source // 128).astype(jnp.float32).astype(jnp.bfloat16)
+    moved[...] = (target == 4 * (source % 128) + source // 128).astype(jnp.float32).astype(jnp.bfloat16)
+
+
+def placed_features(pooled, moved):
+    count = pooled.shape[0]
     stacked = jnp.concatenate([piece.astype(jnp.bfloat16) for piece in pieces(pooled)], axis=0)
-    placed = jnp.dot(stacked, moved, preferred_element_type=jnp.float32)
-    block[:count, :] = placed[:count] + placed[count:2 * count] + placed[2 * count:]
-    block[count:, :] = jnp.zeros((8, order), jnp.float32)
+    placed = jnp.dot(stacked, moved[...], preferred_element_type=jnp.float32)
+    return placed[:count] + placed[count:2 * count] + placed[2 * count:]
+
+
+def feature_scratch(count, plane):
+    return [
+        pltpu.VMEM((4, 256, 512), jnp.bfloat16),
+        pltpu.VMEM((7, plane // BAND * count, BAND), jnp.bfloat16),
+        pltpu.VMEM((512, 512), jnp.bfloat16),
+    ]
+
+
+def features_kernel(images, seeds, labels, block, weights, windows, moved):
+    count = images.shape[0]
+    make_weights(seeds, weights)
+    make_order(moved)
+    make_windows(images, windows)
+    block[:count, :] = placed_features(pooled_features(count, weights, windows), moved)
+    block[count:, :] = jnp.zeros((8, block.shape[1]), jnp.float32)
     block[count:count + 1, :count] = labels[...].astype(jnp.float32)
 
 
 def features_block(images, labels, seeds):
     count, pixels = images.shape
-    order = 4 * seeds.shape[0]
-    windows = (pixels // 3 - 256) // 128 + 1
     vmem = pl.BlockSpec(memory_space=pltpu.VMEM)
     return pl.pallas_call(
         features_kernel,
-        out_shape=jax.ShapeDtypeStruct((count + 8, order), jnp.float32),
+        out_shape=jax.ShapeDtypeStruct((count + 8, 4 * seeds.shape[0]), jnp.float32),
         in_specs=[vmem] * 3,
         out_specs=vmem,
-        scratch_shapes=[
-            pltpu.VMEM((windows * count, 768), jnp.bfloat16),
-            pltpu.VMEM((8, 96 + 768, 128), jnp.float32),
-            pltpu.VMEM((8, 96 + 768, 128), jnp.bfloat16),
-        ],
+        scratch_shapes=feature_scratch(count, pixels // 3),
         compiler_params=pltpu.CompilerParams(vmem_limit_bytes=24 * 1024 * 1024),
         name="features",
     )(images, seeds[None, :], labels[None, :])

time: 58 us -> 54.8 us (0.945)
  Pallas kernels: 55.2 us -> 52 us
    pallas_call x1, Pallas kernels: 5.59 us -> 2.43 us  [features_block(): pl.pallas_call(features_kernel, out_shape=jax.ShapeDtypeStruct((count + 8...]
where the time goes in v2:
time: 54.8 us; the launch traced here: 54.7 us
  Pallas kernels  52 us (95%)
  local copies, waits for them, and re-layouts  1.79 us (3%)
  between operations  0.82 us (1%)
    pallas_call x1, Pallas kernels, gathered_sums(): pl.pallas_call(lambda *refs: gather_kernel(span, ridge, *refs), out_shape...  34 us
    pallas_call x1, Pallas kernels, factor(): pl.pallas_call(factor_kernel, out_shape=(jax.ShapeDtypeStruct(gram.shape,...  15.6 us
    pallas_call x1, Pallas kernels, features_block(): pl.pallas_call(features_kernel, out_shape=jax.ShapeDtypeStruct((count + 8...  2.43 us
    unnamed x6, local copies, waits for them, and re-layouts  1.79 us

profile of v2, /device:TPU:1, one launch (start us, length us, event | category | flops | bytes accessed | tf_op | source)
XLA Modules:
  0.0 54.7 jit_solution(7845345564932498134)
XLA Ops:
  0.6 0.0 copy-start.1
  0.6 0.0 copy-start.2
  0.6 0.6 %copy-done.1 = s32[128]{0:T(128)S(1)} copy-done((s32[128]{0:T(128)S(1)}, s32[128]{0:T(128)}, u32[]{:S(2)}) %copy-start.1) | copy-done | bytes 536
  1.3 0.0 copy-done.2
  1.3 0.0 copy-start
  1.3 1.1 %copy-done = bf16[128,3072]{1,0:T(8,128)(2,1)S(1)} copy-done((bf16[128,3072]{1,0:T(8,128)(2,1)S(1)}, bf16[128,3072]{1,0:T(8,128)(2,1)}, u32[]{:S(2)}) %copy-start) | copy-done | bytes 786456
  2.4 2.4 %features.1.refs_0_ = f32[136,512]{1,0:T(8,128)S(1)} custom-call(bf16[128,3072]{1,0:T(8,128)(2,1)S(1)} %copy-done, s32[1,128]{1,0:T(1,128)S(1)} %bitcast.3, s32[1,128]{1,0:T(1,128)S(1)} %bitcast.4), custom_call_target="tpu_custom_call" | custom-call | tf_op jit(solution)/shard_map/features/pallas_call | solution.py:238
  4.9 34.0 %gather_sums.1 = (f32[512,512]{1,0:T(8,128)S(1)}, f32[500,512]{1,0:T(8,128)S(1)}) custom-call(f32[136,512]{1,0:T(8,128)S(1)} %features.1.refs_0_), custom_call_target="tpu_custom_call" | custom-call | tf_op jit(solution)/shard_map/gather_sums/pallas_call | solution.py:408
  38.9 15.6 %factor.1 = (f32[512,512]{1,0:T(8,128)}, f32[500,512]{1,0:T(8,128)}) custom-call(f32[512,512]{1,0:T(8,128)S(1)} %get-tuple-element.6.gram, f32[500,512]{1,0:T(8,128)S(1)} %get-tuple-element.7.sums), custom_call_target="tpu_custom_call" | custom-call | tf_op jit(solution)/shard_map/factor/pallas_call | solution.py:128
Async XLA Ops:
  0.6 0.7 %copy-start.1 = (s32[128]{0:T(128)S(1)}, s32[128]{0:T(128)}, u32[]{:S(2)}) copy-start(s32[128]{0:T(128)} %param.5) | copy-start | bytes 1540
  0.6 0.7 %copy-start.2 = (s32[128]{0:T(128)S(1)}, s32[128]{0:T(128)}, u32[]{:S(2)}) copy-start(s32[128]{0:T(128)} %param.4) | copy-start | bytes 1540
  1.3 1.1 %copy-start = (bf16[128,3072]{1,0:T(8,128)(2,1)S(1)}, bf16[128,3072]{1,0:T(8,128)(2,1)}, u32[]{:S(2)}) copy-start(bf16[128,3072]{1,0:T(8,128)(2,1)} %images.1) | copy-start | bytes 2359300

commit v3 on v2

--- a/solution.py
+++ b/solution.py
@@ -11,6 +11,7 @@
 RIDGE = 0.001
 PANEL = 128
 STRIP = 32
+LEAD = 8
 BAND = 128
 GATHER_LIMIT = 16 * 1024 * 1024
 HIGHEST = lax.Precision.HIGHEST
@@ -46,11 +47,11 @@
     for base in range(0, PANEL, STRIP):
         rows = [work[base + 8 * h:base + 8 * h + 8, :] for h in range(tiles)]
         cols = {}
-        for j in range(STRIP):
-            for h in range(j // 8, tiles):
-                cols[j, h] = jnp.broadcast_to(rows[h][:, base + j:base + j + 1], (8, PANEL))
         scale = [None] * tiles
         for k in range(0, STRIP, 2):
+            for j in range(0 if k == 0 else k + LEAD, min(k + LEAD + 2, STRIP)):
+                for h in range(j // 8, tiles):
+                    cols[j, h] = jnp.broadcast_to(rows[h][:, base + j:base + j + 1], (8, PANEL))
             own, row = divmod(k, 8)
             one = spread(cols[k, own], row)
             cross = spread(cols[k, own], row + 1)
@@ -69,7 +70,7 @@
                 if h == own:
                     first[h] = jnp.where(sub > row, first[h], 0.0)
                     second[h] = jnp.where(sub > row + 1, second[h], 0.0)
-            for j in range(k + 2, STRIP):
+            for j in range(k + 2, min(k + LEAD + 2, STRIP)):
                 peer, place = divmod(j, 8)
                 entry = spread(cols[k, peer], place)
                 other = spread(rest[peer], place)
@@ -222,28 +223,25 @@
     ]
 
 
-def features_kernel(images, seeds, labels, block, weights, windows, moved):
-    count = images.shape[0]
+def features_kernel(images, seeds, block, weights, windows, moved):
     make_weights(seeds, weights)
     make_order(moved)
     make_windows(images, windows)
-    block[:count, :] = placed_features(pooled_features(count, weights, windows), moved)
-    block[count:, :] = jnp.zeros((8, block.shape[1]), jnp.float32)
-    block[count:count + 1, :count] = labels[...].astype(jnp.float32)
-
-
-def features_block(images, labels, seeds):
+    block[...] = placed_features(pooled_features(images.shape[0], weights, windows), moved)
+
+
+def features_block(images, seeds):
     count, pixels = images.shape
     vmem = pl.BlockSpec(memory_space=pltpu.VMEM)
     return pl.pallas_call(
         features_kernel,
-        out_shape=jax.ShapeDtypeStruct((count + 8, 4 * seeds.shape[0]), jnp.float32),
-        in_specs=[vmem] * 3,
+        out_shape=jax.ShapeDtypeStruct((count, 4 * seeds.shape[0]), jnp.float32),
+        in_specs=[vmem] * 2,
         out_specs=vmem,
         scratch_shapes=feature_scratch(count, pixels // 3),
         compiler_params=pltpu.CompilerParams(vmem_limit_bytes=24 * 1024 * 1024),
         name="features",
-    )(images, seeds[None, :], labels[None, :])
+    )(images, seeds[None, :])
 
 
 def visit(here, step, length):
@@ -260,15 +258,20 @@
     return 0, early, middle, rows
 
 
-def gather_kernel(span, ridge, block, gram, sums, held, local_sem, send_sem, recv_sem):
+def gather_kernel(span, ridge, images, seeds, labels, gram, sums, picture, seed_row, label_row, weights, windows, moved, held,
+                  local_sem, send_sem, recv_sem):
     wide, deep = span
     x, z, c = lax.axis_index("sub"), lax.axis_index("img"), lax.axis_index("cls")
     across, other = wide - 1 - x, 1 - c
-    count, order = block.shape[0] - 8, block.shape[1]
-    classes = sums.shape[0]
+    count, order, classes = picture.shape[0], gram.shape[0], sums.shape[0]
     has_up, has_down = z < deep - 1, z > 0
     targets = ({"img": z + 1}, {"img": z - 1}, {"sub": across}, {"cls": other})
 
+    loads = [pltpu.make_async_copy(seeds, seed_row, local_sem.at[0]),
+             pltpu.make_async_copy(images, picture, local_sem.at[1]),
+             pltpu.make_async_copy(labels, label_row, local_sem.at[2])]
+    for load in loads:
+        load.start()
     barrier = pltpu.get_barrier_semaphore()
     for exists, target in zip((has_up, has_down, True, True), targets):
         if exists is True:
@@ -277,14 +280,20 @@
             @pl.when(exists)
             def _():
                 pl.semaphore_signal(barrier, inc=1, device_id=target, device_id_type=MESH)
-    own = pltpu.make_async_copy(block, held.at[x, z, c], local_sem.at[0])
-    own.start()
+    make_order(moved)
     gram[...] = jnp.zeros_like(gram)
     sums[...] = jnp.zeros_like(sums)
+    loads[0].wait()
+    make_weights(seed_row, weights)
+    loads[1].wait()
+    make_windows(picture, windows)
+    held[x, z, c, :count, :] = placed_features(pooled_features(count, weights, windows), moved)
+    loads[2].wait()
+    held[x, z, c, count:, :] = jnp.zeros((8, order), jnp.float32)
+    held[x, z, c, count:count + 1, :count] = label_row[...].astype(jnp.float32)
     pl.semaphore_wait(barrier, 2 + has_up.astype(jnp.int32) + has_down.astype(jnp.int32))
-    own.wait()
-
-    cuts = piece_cuts(block.shape[0], deep)
+
+    cuts = piece_cuts(count + 8, deep)
 
     def copy(way, i, j, k, piece):
         slot = held.at[i, j, k, pl.ds(cuts[piece], cuts[piece + 1] - cuts[piece])]
@@ -402,23 +411,28 @@
                 copy(2, x, j, c, piece).wait_send()
 
 
-def gathered_sums(block, span, ridge, classes):
-    order = block.shape[1]
-    vmem = pl.BlockSpec(memory_space=pltpu.VMEM)
+def gathered_sums(images, seeds, labels, span, ridge, classes):
+    count, pixels = images.shape
+    order = 4 * seeds.shape[0]
+    vmem, far = pl.BlockSpec(memory_space=pltpu.VMEM), pl.BlockSpec(memory_space=pltpu.MemorySpace.HBM)
     return pl.pallas_call(
         lambda *refs: gather_kernel(span, ridge, *refs),
         out_shape=(jax.ShapeDtypeStruct((order, order), jnp.float32), jax.ShapeDtypeStruct((classes, order), jnp.float32)),
-        in_specs=[vmem],
+        in_specs=[far] * 3,
         out_specs=(vmem, vmem),
         scratch_shapes=[
-            pltpu.VMEM((*span, 2, *block.shape), jnp.float32),
-            pltpu.SemaphoreType.DMA((1,)),
+            pltpu.VMEM((count, pixels), jnp.bfloat16),
+            pltpu.VMEM((1, seeds.shape[0]), jnp.int32),
+            pltpu.VMEM((1, count), jnp.int32),
+            *feature_scratch(count, pixels // 3),
+            pltpu.VMEM((*span, 2, count + 8, order), jnp.float32),
+            pltpu.SemaphoreType.DMA((3,)),
             pltpu.SemaphoreType.DMA((4, *span, 3)),
             pltpu.SemaphoreType.DMA((*span, 2, 3)),
         ],
         compiler_params=pltpu.CompilerParams(collective_id=0, has_side_effects=True, vmem_limit_bytes=32 * 1024 * 1024),
         name="gather_sums",
-    )(block)
+    )(*(pltpu.with_memory_space_constraint(v, pltpu.MemorySpace.HBM) for v in (images, seeds[None, :], labels[None, :])))
 
 
 def reduced_sums(feats, labels, ridge):
@@ -436,16 +450,14 @@
 
 def shards(images, labels, seeds):
     count = images.shape[0]
-    block = features_block(images, labels, seeds)
-    order = block.shape[1]
     span = (lax.axis_size("sub"), lax.axis_size("img"))
     pair = lax.axis_size("cls")
     ridge = RIDGE * count * span[0] * span[1] * pair
-    held_bytes = span[0] * span[1] * pair * block.size * 4
+    held_bytes = span[0] * span[1] * pair * (count + 8) * 16 * seeds.shape[0]
     if span[0] == 2 and span[1] > 1 and pair == 2 and count == 128 and held_bytes <= GATHER_LIMIT:
-        gram, sums = gathered_sums(block, span, ridge, CLASSES // pair)
+        gram, sums = gathered_sums(images, seeds, labels, span, ridge, CLASSES // pair)
     else:
-        gram, sums = reduced_sums(block[:count], labels, ridge)
+        gram, sums = reduced_sums(features_block(images, seeds), labels, ridge)
     rfactor, projections = factor(gram, sums)
     return rfactor, projections.T
 

time: 54.8 us -> 50.4 us (0.920)
  Pallas kernels: 52 us -> 49.4 us
  local copies, waits for them, and re-layouts: 1.79 us -> 0 us
    pallas_call x1, Pallas kernels: 15.6 us -> 13.1 us  [factor(): pl.pallas_call(factor_kernel, out_shape=(jax.ShapeDtypeStruct(gram.shape,...]
    pallas_call x1 -> x0, Pallas kernels: 2.43 us -> none  [features_block(): pl.pallas_call(features_kernel, out_shape=jax.ShapeDtypeStruct((count + 8...]
    pallas_call x1, Pallas kernels: 34 us -> 36.3 us  [gathered_sums(): pl.pallas_call(lambda *refs: gather_kernel(span, ridge, *refs), out_shape...]
    unnamed x6 -> x0, local copies, waits for them, and re-layouts: 1.79 us -> none
where the time goes in v3:
time: 50.4 us; the launch traced here: 50.2 us
  Pallas kernels  49.4 us (98%)
  between operations  0.8 us (2%)
    pallas_call x1, Pallas kernels, gathered_sums(): pl.pallas_call(lambda *refs: gather_kernel(span, ridge, *refs), out_shape...  36.3 us
    pallas_call x1, Pallas kernels, factor(): pl.pallas_call(factor_kernel, out_shape=(jax.ShapeDtypeStruct(gram.shape,...  13.1 us

profile of v3, /device:TPU:1, one launch (start us, length us, event | category | flops | bytes accessed | tf_op | source)
XLA Modules:
  0.0 50.2 jit_solution(15578063121740348446)
XLA Ops:
  0.6 36.3 %gather_sums.1 = (f32[512,512]{1,0:T(8,128)S(1)}, f32[500,512]{1,0:T(8,128)S(1)}) custom-call(bf16[128,3072]{1,0:T(8,128)(2,1)} %refs_0_.1, s32[1,128]{1,0:T(1,128)} %bitcast.3, s32[1,128]{1,0:T(1,128)} %bitcast.4), custom_call_target="tpu_custom_call" | custom-call | tf_op jit(solution)/shard_map/gather_sums/pallas_call | solution.py:418
  36.9 13.1 %factor.1 = (f32[512,512]{1,0:T(8,128)}, f32[500,512]{1,0:T(8,128)}) custom-call(f32[512,512]{1,0:T(8,128)S(1)} %get-tuple-element.6.gram, f32[500,512]{1,0:T(8,128)S(1)} %get-tuple-element.7.sums), custom_call_target="tpu_custom_call" | custom-call | tf_op jit(solution)/shard_map/factor/pallas_call | solution.py:129
